TPU v7x, 256 devices: a whole 4x4x8 slice. The times are simulated.
256 devices in a mesh: fsdp: 32 (over x_lo, z, core), proto: 4 (over y), dp: 2 (over x_hi).
Axes of the slice: x: 4 (x_hi: 2, x_lo: 2; x = x_hi * 2 + x_lo), y: 4, z: 8, core: 2. Of those that a mesh axis runs over, the one named last changes fastest.
Arguments:
- teacher_weight: float32 [192, 65536], P(None, ('proto', 'fsdp')), may hold values from -0.4375 to 0.4375
- student_weight: float32 [192, 65536], P(None, ('proto', 'fsdp')), may hold values from -0.4375 to 0.4375
- teacher_feats: bfloat16 [2, 8192, 192], P('dp', 'fsdp'), may hold values from -6 to 6
- student_feats: bfloat16 [2, 8192, 192], P('dp', 'fsdp'), may hold values from -6 to 6
- pairing: int32 [2, 8192], P('dp', 'fsdp'), may hold values from 0 to 255
- center: float32 [65536], P('proto'), may hold values from -10.3 to -3.7
Outputs:
- teacher_new: float32 [192, 65536], P(None, ('proto', 'fsdp'))
- student_grad: float32 [192, 65536], P(None, ('proto', 'fsdp', 'dp'))
Inputs may be any that keep to these rules, and one draw needn't show every extreme that they name: pairing[v, r] indexes a crop of the other view in the same block of 256 crops.
All inputs are finite; a program needn't handle non-finite values.
Results may differ from a plain program's by a relative error of at most 0.012.
Values may be sent and summed in bfloat16 or wider, within the bound.
A program may use at most 128 MiB of HBM per device.

v0:
```python
import jax
import jax.numpy as jnp
from jax import lax
from jax.sharding import PartitionSpec as P


def from_partner(shard, axis, apart):
    return lax.ppermute(shard, axis, [(i, i ^ 1 << apart) for i in range(lax.axis_size(axis))])


def normalize_cols(weights):
    return weights * lax.rsqrt(jnp.sum(weights * weights, axis=0, keepdims=True) + 1e-06)


def normalize_rows(feats):
    values = feats.astype(jnp.float32)
    return values * lax.rsqrt(jnp.sum(values * values, axis=-1, keepdims=True) + 1e-06)


def shards(teacher_weight, student_weight, teacher_feats, student_feats, pairing, center):
    teacher_new = 0.994 * teacher_weight + 0.006 * student_weight
    w_teacher = normalize_cols(teacher_new).astype(jnp.bfloat16)
    w_student = normalize_cols(student_weight).astype(jnp.bfloat16)
    z_teacher = normalize_rows(teacher_feats[0]).astype(jnp.bfloat16)
    z_student = normalize_rows(student_feats[0]).astype(jnp.bfloat16)
    swapped = from_partner(z_teacher, "dp", 0)
    paired = jnp.take(swapped, pairing[0], axis=0)
    logits_t = jnp.dot(
        paired,
        lax.all_gather(w_teacher, "fsdp", axis=1, tiled=True),
        preferred_element_type=jnp.float32,
    )
    logits_s = jnp.dot(
        z_student,
        lax.all_gather(w_student, "fsdp", axis=1, tiled=True),
        preferred_element_type=jnp.float32,
    )
    scores_t = (logits_t - center[None, :]) / 0.04
    scores_s = logits_s / 0.1
    local_max_t = jnp.max(scores_t, axis=1)
    local_max_s = jnp.max(scores_s, axis=1)
    max_t, max_s = lax.pmax((local_max_t, local_max_s), "proto")
    exp_t = jnp.exp(scores_t - max_t[:, None])
    exp_s = jnp.exp(scores_s - max_s[:, None])
    total_t, total_s = lax.psum((jnp.sum(exp_t, axis=1), jnp.sum(exp_s, axis=1)), "proto")
    derivs = ((exp_s / total_s[:, None] - exp_t / total_t[:, None]) / 0.1).astype(jnp.bfloat16)
    grad_rows_mine = lax.psum_scatter(
        lax.dot_general(
            derivs, z_student, (((0,), (0,)), ((), ())), preferred_element_type=jnp.float32
        ),
        ("fsdp", "dp"),
        scatter_dimension=0,
        tiled=True,
    )
    grad_part = grad_rows_mine.T
    width = grad_part.shape[1]
    offset = lax.axis_index("dp") * width
    student_part = lax.dynamic_slice_in_dim(student_weight, offset, width, 1)
    norms = jnp.sqrt(jnp.sum(student_part * student_part, axis=0, keepdims=True) + 1e-06)
    unit = student_part / norms
    student_grad = (grad_part - unit * jnp.sum(unit * grad_part, axis=0, keepdims=True)) / norms
    return (teacher_new, student_grad)


def solution(mesh):
    placed = (
        P(None, ("proto", "fsdp")),
        P(None, ("proto", "fsdp")),
        P("dp", "fsdp", None),
        P("dp", "fsdp", None),
        P("dp", "fsdp"),
        P("proto"),
    )
    return jax.shard_map(
        shards,
        mesh=mesh,
        in_specs=placed,
        out_specs=(P(None, ("proto", "fsdp")), P(None, ("proto", "fsdp", "dp"))),
        check_vma=False,
    )
```

profile of v0, /device:TPU:1, one launch (start us, length us, event | category | flops | bytes accessed | tf_op | source)
XLA Modules:
  0.0 518.8 jit_solution(17187875234807501835)
XLA Ops:
  7.2 0.0 copy-start.3
  7.2 0.0 all-gather.3.cloned.1.call-start
  7.2 1.0 multiply_reduce_fusion.1
  8.3 1.9 multiply_reduce_fusion
  10.2 0.0 copy-start.1
  10.2 0.0 all-gather.3.cloned.1.call-update
  10.2 0.0 all-gather.5.cloned.1.call-start
  10.3 0.7 multiply_convert_fusion.2
  11.0 0.0 all-gather.5.cloned.1.call-update
  11.0 0.0 reduce-scatter.2.cloned.1.call-start
  11.0 1.0 copy.9
  12.0 0.1 fusion.4
  12.2 0.1 fusion.5
  12.3 3.7 collective-permute-start
  15.9 0.9 fusion.6
  16.9 0.7 compare_and_fusion
  17.6 0.7 compare_select_fusion
  18.3 0.0 collective-permute-done
  18.3 1.2 gather_fusion
  19.5 65.5 %all-gather.3.cloned.1.call-done = bf16[192,16384]{1,0:T(8,128)(2,1)} async-done(((bf16[192,512]{1,0:T(8,128)(2,1)}), bf16[192,16384]{1,0:T(8,128)(2,1)}) %all-gather.3.cloned.1.call-update) | async-done | bytes 6291472 | tf_op jit(solution)/shard_map/all_gather | solution.py:35
  84.9 11.0 %fusion.18 = (f32[256]{0:T(256)S(1)}, f32[256,16384]{1,0:T(8,128)}) fusion(bf16[192,16384]{1,0:T(8,128)(2,1)} %all-gather.3.cloned.1.call-done, bf16[1,256,192]{1,2,0:T(8,128)(2,1)} %param.9, f32[256]{0:T(256)S(1)} %add_rsqrt_fusion.3), kind=kOutput, calls=%fused_computation.44 | convolution fusion | flops 1619148544 | bytes 23169024 | tf_op jit(solution)/shard_map/dot_general | solution.py:33
  95.9 61.0 %all-gather.5.cloned.1.call-done = bf16[192,16384]{1,0:T(8,128)(2,1)} async-done(((bf16[192,512]{1,0:T(8,128)(2,1)}), bf16[192,16384]{1,0:T(8,128)(2,1)}) %all-gather.5.cloned.1.call-update) | async-done | bytes 6291472 | tf_op jit(solution)/shard_map/all_gather | solution.py:30
  156.9 0.0 copy-done.3
  156.9 10.0 %fusion.17 = (f32[256]{0:T(256)S(1)}, f32[256,16384]{1,0:T(8,128)}) fusion(f32[16384]{0:T(1024)S(1)} %copy-done.3, bf16[192,16384]{1,0:T(8,128)(2,1)} %all-gather.5.cloned.1.call-done, bf16[256,192]{1,0:T(8,128)(2,1)S(1)} %gather_fusion, pred[256]{0:T(512)(128)(4,1)S(1)} %compare_and_fusion), kind=kOutput, calls=%fused_computation.43 | convolution fusion | flops 1623244544 | bytes 23233792 | tf_op jit(solution)/shard_map/dot_general | solution.py:28
  166.9 0.0 copy-done.1
  166.9 8.4 %all-reduce.1 = (f32[256]{0:T(256)S(1)}, f32[256]{0:T(256)S(1)}) all-reduce(f32[256]{0:T(256)S(1)} %get-tuple-element.9, f32[256]{0:T(256)S(1)} %get-tuple-element.11), channel_id=1, replica_groups=mesh['fsdp'=32,'proto'=4,'dp'=2] {'proto'}, use_global_device_ids=true, to_apply=%region_9.10 | all-reduce | flops 512 | bytes 4096 | tf_op jit(solution)/shard_map/pmax | solution.py:42
  175.3 0.0 copy-start.2
  175.3 12.2 %fusion.1 = (f32[256]{0:T(256)S(1)}, f32[256]{0:T(256)S(1)}) fusion(f32[256,16384]{1,0:T(8,128)} %get-tuple-element.12, f32[256]{0:T(256)S(1)} %get-tuple-element.5, f32[256,16384]{1,0:T(8,128)} %get-tuple-element.10, f32[256]{0:T(256)S(1)} %get-tuple-element.4), kind=kLoop, calls=%fused_computation.7 | loop fusion | flops 16776704 | bytes 33558528 | tf_op jit(solution)/shard_map/reduce_sum | solution.py:45
  187.5 6.0 %all-reduce = (f32[256]{0:T(256)S(1)}, f32[256]{0:T(256)S(1)}) all-reduce(f32[256]{0:T(256)S(1)} %get-tuple-element.14, f32[256]{0:T(256)S(1)} %get-tuple-element.13), channel_id=1, replica_groups=mesh['fsdp'=32,'proto'=4,'dp'=2] {'proto'}, use_global_device_ids=true, to_apply=%region_11.12 | all-reduce | flops 512 | bytes 4096 | tf_op jit(solution)/shard_map/psum | solution.py:45
  193.5 0.0 copy-done.2
  193.5 0.0 copy-start
  193.5 17.4 %fusion.3 = f32[16384,192]{0,1:T(8,128)} fusion(f32[256,16384]{1,0:T(8,128)} %get-tuple-element.12, f32[256,16384]{1,0:T(8,128)} %get-tuple-element.10, f32[256]{0:T(256)S(1)} %get-tuple-element.2, f32[256]{0:T(256)S(1)} %get-tuple-element.4, f32[256]{0:T(256)S(1)} %get-tuple-element.3, f32[256]{0:T(256)S(1)} %get-tuple-element.5, ...), kind=kOutput, calls=%fused_computation.9 | convolution fusion | flops 1640120320 | bytes 46240768 | tf_op jit(solution)/shard_map/dot_general | solution.py:48
  210.9 0.0 reduce-scatter.2.cloned.1.call-update
  211.0 0.0 copy-done
  211.0 298.6 %reduce-scatter.2.cloned.1.call-done = f32[256,192]{0,1:T(8,128)} async-done(((f32[16384,192]{0,1:T(8,128)}), f32[256,192]{0,1:T(8,128)}) %reduce-scatter.2.cloned.1.call-update) | async-done | bytes 196624 | tf_op jit(solution)/shard_map/reduce_scatter | solution.py:47
  509.6 1.0 fusion.8
  510.6 1.6 fusion.9
  (7 shorter events, 0.1 us)
Async XLA Ops:
  7.2 149.7 %copy-start.3 = (f32[16384]{0:T(1024)S(1)}, f32[16384]{0:T(1024)}, u32[]{:S(2)}) copy-start(f32[16384]{0:T(1024)} %param.11) | copy-start | bytes 196612
  7.2 77.7 %all-gather.3.cloned.1.call-start = ((), (), s32[]{:S(2)}) async-start(), calls=%async_computation.1 | async-start | bytes 6488064 | tf_op jit(solution)/shard_map/all_gather | solution.py:35
  10.2 156.7 %copy-start.1 = (f32[192,512]{1,0:T(8,128)}, f32[192,512]{1,0:T(8,128)S(1)}, u32[]{:S(2)}) copy-start(f32[192,512]{1,0:T(8,128)S(1)} %get-tuple-element.7) | copy-start | bytes 1179652
  10.2 146.7 %all-gather.5.cloned.1.call-start = ((), (), s32[]{:S(2)}) async-start(), calls=%async_computation.2 | async-start | bytes 6488064 | tf_op jit(solution)/shard_map/all_gather | solution.py:30
  11.0 498.6 %reduce-scatter.2.cloned.1.call-start = ((), (), s32[]{:S(2)}) async-start(), calls=%async_computation.3 | async-start | bytes 12779520 | tf_op jit(solution)/shard_map/reduce_scatter | solution.py:47
  12.3 6.0 %collective-permute-start = (bf16[256,192]{1,0:T(8,128)(2,1)S(1)}, bf16[256,192]{1,0:T(8,128)(2,1)S(1)}, u32[]{:S(2)}, u32[]{:S(2)}) collective-permute-start(bf16[256,192]{1,0:T(8,128)(2,1)S(1)} %fusion.5), channel_id=1, source_target_pairs={{0,1},{1,0},{2,3},{3,2},{4,5},{5,4},{6,7},{7,6},{8,9},{9,8},{10,11... | collective-permute-start | bytes 294920 | tf_op jit(solution)/shard_map/ppermute | solution.py:8
  175.3 18.2 %copy-start.2 = (bf16[1,256,192]{1,2,0:T(8,128)(2,1)S(1)}, bf16[1,256,192]{1,2,0:T(8,128)(2,1)}, u32[]{:S(2)}) copy-start(bf16[1,256,192]{1,2,0:T(8,128)(2,1)} %param.9) | copy-start | bytes 294916
  193.5 17.5 %copy-start = (f32[192,512]{1,0:T(8,128)S(1)}, f32[192,512]{1,0:T(8,128)}, u32[]{:S(2)}) copy-start(f32[192,512]{1,0:T(8,128)} %param.7) | copy-start | bytes 1179652
Sparse Core Ops, SparseCore 0:
  10.5 74.4 all-gather.2
  86.8 70.0 all-gather.4
  211.1 298.4 reduce-scatter.1
where the time goes:
time: 519 us
  waiting for transfers between devices  425 us (82%)
  matrix products  38.4 us (7%)
  other arithmetic  21 us (4%)
  blocking collectives  14.4 us (3%)
  between operations  13.8 us (3%)
    reduce_scatter x1, waiting for transfers between devices, shards(): lax.psum_scatter(lax.dot_general(derivs, z_student, (((0,), (0,)), ((), (...  299 us
    all_gather x1, waiting for transfers between devices, shards(): lax.all_gather(w_student, 'fsdp', axis=1, tiled=True)  65.5 us
    all_gather x1, waiting for transfers between devices, shards(): lax.all_gather(w_teacher, 'fsdp', axis=1, tiled=True)  61 us
    dot_general x1, matrix products, shards(): lax.dot_general(derivs, z_student, (((0,), (0,)), ((), ())), preferred_el...  17.4 us
    reduce_sum x1, other arithmetic, shards(): jnp.sum(exp_s, axis=1)  12.2 us
    dot_general x1, matrix products, shards(): jnp.dot(z_student, lax.all_gather(w_student, 'fsdp', axis=1, tiled=True),...  11 us
  transfers between devices with their start and end apart: 4, of which 3 were waited for; matrix products, arithmetic and copies ran while one was open for 3% of the time, Pallas kernels for 0%

commit v1 on v0

v1 whole, which is shorter than its diff:
```python
import math

import jax
import jax.numpy as jnp
import numpy as np
from jax import lax
from jax.experimental import pallas as pl
from jax.experimental.pallas import tpu as pltpu
from jax.sharding import PartitionSpec as P

MESH = pl.DeviceIdType.MESH
F32, BF16 = jnp.float32, jnp.bfloat16
T_SCALE = math.log2(math.e) / 0.04
S_SCALE = math.log2(math.e) / 0.1
EPS = 1e-06


def rem(a, n):
    return lax.rem(a, np.int32(n))


def div(a, n):
    return lax.div(a, np.int32(n))


def device(x, y, z, core):
    return ((rem(x, 2) * 8 + z) * 2 + core, y, div(x, 2))


NAMES = (
    ["wr", "wl", "wr2", "wl2"]
    + [f"ws{i}" for i in range(4)]
    + ["cr", "cl", "c2", "pair"]
    + ["sr1", "sl1", "sr2", "sl2"]
    + [f"sx{w}{j}" for w in ("r", "l", "rr", "ll") for j in range(4)]
    + ["txr", "txl", "txrr", "txll"]
    + [f"tz{w}{j}" for w in ("r1", "l1", "r2", "l2") for j in range(4)]
    + [f"x{t}{i}" for t in range(2) for i in range(3)]
    + [f"z{t}{i}" for t in range(2) for i in range(7)]
    + [f"g{i}" for i in range(4)]
    + ["ra", "rb", "rr", "rl"]
)
INDEX = {name: i for i, name in enumerate(NAMES)}


def kernel(
    tw_ref, sw_ref, tf_ref, sf_ref, pair_ref, cen_ref, tnew_ref, grad_ref,
    wbuf, cbuf, zs, zt, ztl, pair_in, e_buf, cb, tot, xin, xsum, zin, at, g, gs_out, gs_in, ry_out, ra_in, ry_in,
    ssem, rsem,
):
    f, y, d = lax.axis_index("fsdp"), lax.axis_index("proto"), lax.axis_index("dp")
    core, z = rem(f, 2), rem(div(f, 2), 8)
    x = d * 2 + div(f, 16)
    parity, chunk = div(y, 2), rem(y, 2)
    away = rem(z + 8 - parity, 8)
    q0 = div(away, 2)
    source = rem(away, 2) == 0
    relay = rem(away, 2) == 1

    def at_x(k):
        return rem(x + k, 4)

    def at_y(k):
        return rem(y + k, 4)

    def at_z(k):
        return rem(z + k, 8)

    def to_x(k):
        return device(at_x(k), y, z, core)

    def to_y(k):
        return device(x, at_y(k), z, core)

    def to_z(k):
        return device(x, y, at_z(k), core)

    sibling = device(x, y, z, 1 - core)
    quarter = [rem(q0 + k, 4) for k in (0, 1, 3, 2)]
    sent = {"all": [], "source": [], "relay": []}

    def copy(name, src, dst, to):
        i = INDEX[name]
        return pltpu.make_async_remote_copy(
            src_ref=src, dst_ref=dst, send_sem=ssem.at[i], recv_sem=rsem.at[i], device_id=to, device_id_type=MESH
        )

    def send_to(who, name, src, dst, to):
        copy(name, src, dst, to).start()
        sent[who].append((name, src.shape, src.dtype))

    def send(who, name, ref, to):
        send_to(who, name, ref, ref, to)

    def arrived(name, ref):
        copy(name, ref, ref, sibling).wait_recv()

    peers = [sibling] + [to_y(k) for k in (1, 2, 3)] + [to_x(k) for k in (1, 2, 3)] + [to_z(k) for k in range(1, 8)]
    barrier = pltpu.get_barrier_semaphore()
    for peer in peers:
        pl.semaphore_signal(barrier, inc=1, device_id=peer, device_id_type=MESH)

    half = pl.ds(pl.multiple_of(d * 256, 256), 256)
    s_cols = sw_ref[:, half]
    t_cols = 0.994 * tw_ref[:, half] + 0.006 * s_cols
    ws = s_cols * lax.rsqrt(jnp.sum(s_cols * s_cols, axis=0, keepdims=True) + EPS)
    wt = t_cols * lax.rsqrt(jnp.sum(t_cols * t_cols, axis=0, keepdims=True) + EPS)
    wbuf[y, core] = jnp.concatenate([wt, ws], axis=0).T.astype(BF16)

    lowest = jnp.min(jnp.min(cen_ref[...], axis=0, keepdims=True), axis=1, keepdims=True)
    cbuf[y, 4:5, :] = jnp.broadcast_to(lowest, (1, 128))
    for k in range(4):
        row = 4 * (f - core) + 4 * (k // 2) + 2 * d + k % 2
        cbuf[y, k : k + 1, :] = cen_ref[pl.ds(row, 1), :]
    cbuf[y, 5:8, :] = jnp.zeros((3, 128), F32)

    @pl.when(source)
    def _():
        feats = sf_ref[:, pl.ds(pl.multiple_of(chunk * 128, 128), 128)].astype(F32)
        zs[q0, x] = (feats * lax.rsqrt(jnp.sum(feats * feats, axis=0, keepdims=True) + EPS)).astype(BF16)

    pl.semaphore_wait(barrier, len(peers))

    @pl.when(source)
    def _():
        send_to("source", "pair", pair_ref.at[:, pl.ds(pl.multiple_of(chunk * 128, 128), 128)], pair_in, to_x(2))
        send("source", "sr1", zs.at[q0, x], to_z(1))
        send("source", "sl1", zs.at[q0, x], to_z(7))
        send("source", "sxr0", zs.at[q0, x], to_x(1))
        send("source", "sxl0", zs.at[q0, x], to_x(3))

    own_w = wbuf.at[y, core]
    send("all", "wr", own_w, to_y(1))
    send("all", "wl", own_w, to_y(3))
    for k, name in ((1, "cr"), (3, "cl"), (2, "c2")):
        send("all", name, cbuf.at[y], to_y(k))
    send("all", "ws0", own_w, sibling)

    low, high = pl.ds(0, 96), pl.ds(96, 96)

    @pl.when(source)
    def _():
        feats = tf_ref[...].astype(F32)
        ztl[...] = (feats * lax.rsqrt(jnp.sum(feats * feats, axis=0, keepdims=True) + EPS)).astype(BF16)
        arrived("pair", pair_in)
        picked = lax.broadcasted_iota(jnp.int32, (256, 128), 0) == pair_in[...]
        onehot = jnp.where(picked, 1.0, 0.0).astype(BF16)
        zt[q0, at_x(2)] = jnp.dot(ztl[...], onehot, preferred_element_type=F32).astype(BF16)
        mine = zt.at[q0, at_x(2)]
        send("source", "txr", mine, to_x(1))
        send("source", "txl", mine, to_x(3))
        send("source", "tzr10", mine, to_z(1))
        send("source", "tzl10", mine, to_z(7))

    tnew_ref[...] = 0.994 * tw_ref[...] + 0.006 * sw_ref[...]

    def cross(who, j):
        send(who, f"sxr{j}", zs.at[quarter[j], x], to_x(1))
        send(who, f"sxl{j}", zs.at[quarter[j], x], to_x(3))

    @pl.when(relay)
    def _():
        arrived("sr1", zs.at[quarter[0], x])
        send("relay", "sr1", zs.at[quarter[0], x], to_z(1))
        arrived("sl1", zs.at[quarter[1], x])
        send("relay", "sl1", zs.at[quarter[1], x], to_z(7))
        cross("relay", 0)
        cross("relay", 1)

    first, last = pl.ds(0, 128), pl.ds(128, 128)
    arrived("wr", wbuf.at[at_y(3), core])
    send("all", "wr2", wbuf.at[at_y(3), core, first], to_y(1))
    arrived("wl", wbuf.at[at_y(1), core])
    send("all", "wl2", wbuf.at[at_y(1), core, last], to_y(3))
    send("all", "ws1", wbuf.at[at_y(3), core], sibling)
    send("all", "ws2", wbuf.at[at_y(1), core], sibling)

    @pl.when(source)
    def _():
        arrived("sr1", zs.at[quarter[2], x])
        send("source", "sr2", zs.at[quarter[2], x], to_z(1))
        arrived("sl1", zs.at[quarter[1], x])
        send("source", "sl2", zs.at[quarter[1], x], to_z(7))
        cross("source", 1)
        cross("source", 2)
        arrived("txr", zt.at[q0, at_x(1)])
        send("source", "txrr", zt.at[q0, at_x(1), low], to_x(1))
        arrived("txl", zt.at[q0, at_x(3)])
        send("source", "txll", zt.at[q0, at_x(3), high], to_x(3))
        for j, k in ((1, 1), (2, 3)):
            send("source", f"tzr1{j}", zt.at[q0, at_x(k)], to_z(1))
            send("source", f"tzl1{j}", zt.at[q0, at_x(k)], to_z(7))

    @pl.when(relay)
    def _():
        arrived("sr2", zs.at[quarter[2], x])
        send("relay", "sr2", zs.at[quarter[2], x, low], to_z(1))
        arrived("sl2", zs.at[quarter[3], x])
        send("relay", "sl2", zs.at[quarter[3], x, high], to_z(7))
        cross("relay", 2)
        cross("relay", 3)

    @pl.when(source)
    def _():
        arrived("txrr", zt.at[q0, x, low])
        arrived("txll", zt.at[q0, x, high])
        send("source", "tzr13", zt.at[q0, x], to_z(1))
        send("source", "tzl13", zt.at[q0, x], to_z(7))
        arrived("sr2", zs.at[quarter[3], x, low])
        arrived("sl2", zs.at[quarter[3], x, high])
        cross("source", 3)

    opposite = wbuf.at[at_y(2), core]
    arrived("wr2", wbuf.at[at_y(2), core, first])
    arrived("wl2", wbuf.at[at_y(2), core, last])
    send("all", "ws3", opposite, sibling)

    for j in range(4):
        arrived(f"sxr{j}", zs.at[quarter[j], at_x(3)])
        send("all", f"sxrr{j}", zs.at[quarter[j], at_x(3), low], to_x(1))
        arrived(f"sxl{j}", zs.at[quarter[j], at_x(1)])
        send("all", f"sxll{j}", zs.at[quarter[j], at_x(1), high], to_x(3))

    across = [at_x(2), at_x(1), at_x(3), x]

    @pl.when(relay)
    def _():
        for j in range(4):
            arrived(f"tzr1{j}", zt.at[quarter[0], across[j]])
            send("relay", f"tzr1{j}", zt.at[quarter[0], across[j]], to_z(1))
            arrived(f"tzl1{j}", zt.at[quarter[1], across[j]])
            send("relay", f"tzl1{j}", zt.at[quarter[1], across[j]], to_z(7))

    for k, name in ((3, "cr"), (1, "cl"), (2, "c2")):
        arrived(name, cbuf.at[at_y(k)])
    floor = jnp.minimum(
        jnp.minimum(cbuf[0, 4:5, :], cbuf[1, 4:5, :]), jnp.minimum(cbuf[2, 4:5, :], cbuf[3, 4:5, :])
    )
    for k in range(16):
        row = (cbuf[k // 4, k % 4 : k % 4 + 1, :] - floor) * T_SCALE
        cb[k * 128 : (k + 1) * 128, :] = jnp.broadcast_to(row, (128, 128)).T

    for i, k in ((0, 0), (1, 3), (2, 1), (3, 2)):
        arrived(f"ws{i}", wbuf.at[at_y(k), 1 - core])
    for j in range(4):
        arrived(f"sxrr{j}", zs.at[quarter[j], at_x(2), low])
        arrived(f"sxll{j}", zs.at[quarter[j], at_x(2), high])

    def scores(which, q, pair):
        z_ref = zs if which else zt
        rhs = jnp.concatenate([z_ref[q, 2 * pair], z_ref[q, 2 * pair + 1]], axis=1)
        pad = jnp.zeros((64, 256), BF16)
        rhs = jnp.concatenate([pad, rhs] if which else [rhs, pad], axis=0)
        lanes = pl.ds(pl.multiple_of(which * 2048 + q * 512 + pair * 256, 256), 256)
        total = jnp.zeros((8, 256), F32)
        for m in range(8):
            rows = pl.ds(m * 256, 256)
            w = wbuf[m // 2, m % 2, :, which * 128 : which * 128 + 256]
            score = jnp.dot(w, rhs, preferred_element_type=F32)
            if which:
                value = jnp.exp2(score * S_SCALE)
            else:
                shift = cb[rows, :]
                value = jnp.exp2(score * T_SCALE - jnp.concatenate([shift, shift], axis=1))
            e_buf[rows, lanes] = value.astype(BF16)
            total = total + jnp.sum(value.reshape(32, 8, 256), axis=0)
        tot[which, pl.ds(q * 2 + pair, 1), :] = jnp.sum(total, axis=0, keepdims=True)

    def loop(low_i, high_i, body):
        lax.fori_loop(low_i, high_i, lambda i, _: body(i), None)

    def student(i):
        scores(1, div(i, 2), rem(i, 2))

    loop(0, 8, student)

    def first_sum(t):
        for i in range(3):
            send_to("all", f"x{t}{i}", tot.at[t], xin.at[t, i], to_x(i + 1))

    def second_sum(t):
        for i in range(3):
            arrived(f"x{t}{i}", xin.at[t, i])
        xsum[t] = tot[t] + xin[t, 0] + xin[t, 1] + xin[t, 2]
        for i in range(7):
            send_to("all", f"z{t}{i}", xsum.at[t], zin.at[t, i], to_z(i + 1))

    def last_sum(t):
        for i in range(7):
            arrived(f"z{t}{i}", zin.at[t, i])
        whole = xsum[t]
        for i in range(7):
            whole = whole + zin[t, i]
        factor = (10.0 if t else -10.0) / whole
        for i in range(8):
            z2 = jnp.concatenate([zs[i // 2, 2 * (i % 2)], zs[i // 2, 2 * (i % 2) + 1]], axis=1).astype(F32)
            at[t, :, i * 256 : (i + 1) * 256] = (z2 * factor[i : i + 1, :]).astype(BF16)

    first_sum(1)

    @pl.when(source)
    def _():
        for j in range(4):
            arrived(f"tzr1{j}", zt.at[quarter[2], across[j]])
            send("source", f"tzr2{j}", zt.at[quarter[2], across[j]], to_z(1))
            arrived(f"tzl1{j}", zt.at[quarter[1], across[j]])
            send("source", f"tzl2{j}", zt.at[quarter[1], across[j]], to_z(7))

    def teacher(q):
        loop(0, 2, lambda i: scores(0, q, i))

    loop(0, 2, lambda i: teacher(rem(q0 + i, 4)))

    @pl.when(relay)
    def _():
        for j in range(4):
            arrived(f"tzr2{j}", zt.at[quarter[2], across[j]])
            if j < 2:
                send("relay", f"tzr2{j}", zt.at[quarter[2], across[j]], to_z(1))
            arrived(f"tzl2{j}", zt.at[quarter[3], across[j]])
            if j >= 2:
                send("relay", f"tzl2{j}", zt.at[quarter[3], across[j]], to_z(7))

    second_sum(1)
    teacher(quarter[2])

    @pl.when(source)
    def _():
        for j in range(4):
            arrived(f"tzr2{j}" if j < 2 else f"tzl2{j}", zt.at[quarter[3], across[j]])

    teacher(quarter[3])
    first_sum(0)
    last_sum(1)

    def term(t, m):
        return lax.dot_general(
            e_buf[pl.ds(pl.multiple_of(m * 256, 256), 256), t * 2048 : (t + 1) * 2048],
            at[t],
            (((1,), (1,)), ((), ())),
            preferred_element_type=F32,
        )

    def student_term(m):
        g[m] = term(1, m)

    loop(0, 3, student_term)
    second_sum(0)
    loop(3, 8, student_term)
    last_sum(0)

    for i, k in enumerate((2, 1, 3, 0)):
        owner = at_y(k)
        theirs, ours = owner * 2 + 1 - core, owner * 2 + core
        gs_out[i] = g[theirs] + term(0, theirs)
        send_to("all", f"g{i}", gs_out.at[i], gs_in.at[i], sibling)
        part = g[ours] + term(0, ours)
        arrived(f"g{i}", gs_in.at[i])
        part = part + gs_in[i]
        if k == 2:
            ry_out[0] = part.astype(BF16)
            send_to("all", "ra", ry_out.at[0, first], ra_in.at[0], to_y(1))
            send_to("all", "rb", ry_out.at[0, last], ra_in.at[1], to_y(3))
        elif k == 1:
            arrived("ra", ra_in.at[0])
            ry_out[1, 0:128] = (part[0:128] + ra_in[0].astype(F32)).astype(BF16)
            ry_out[1, 128:256] = part[128:256].astype(BF16)
            send_to("all", "rr", ry_out.at[1], ry_in.at[0], to_y(1))
        elif k == 3:
            arrived("rb", ra_in.at[1])
            ry_out[2, 0:128] = part[0:128].astype(BF16)
            ry_out[2, 128:256] = (part[128:256] + ra_in[1].astype(F32)).astype(BF16)
            send_to("all", "rl", ry_out.at[2], ry_in.at[1], to_y(3))
        else:
            arrived("rr", ry_in.at[0])
            arrived("rl", ry_in.at[1])
            part = part + ry_in[0].astype(F32) + ry_in[1].astype(F32)
            whole = jnp.concatenate([part, jnp.zeros((256, 64), F32)], axis=1).T[0:192]
            cols = sw_ref[:, half]
            norms = jnp.sqrt(jnp.sum(cols * cols, axis=0, keepdims=True) + EPS)
            unit = cols / norms
            grad_ref[...] = (whole - unit * jnp.sum(unit * whole, axis=0, keepdims=True)) / norms

    some = [
        zs.at[0, 0], zs.at[0, 0, low], wbuf.at[0, 0], wbuf.at[0, 0, first], cbuf.at[0], pair_in, tot.at[0], gs_out.at[0],
        ry_out.at[0], ra_in.at[0],
    ]
    like = {(ref.shape, ref.dtype): ref for ref in some}

    def all_left(who):
        for name, shape, dtype in sent[who]:
            ref = like[shape, dtype]
            copy(name, ref, ref, sibling).wait_send()

    all_left("all")
    pl.when(source)(lambda: all_left("source"))
    pl.when(relay)(lambda: all_left("relay"))


def shards(teacher_weight, student_weight, teacher_feats, student_feats, pairing, center):
    vmem = pl.BlockSpec(memory_space=pltpu.VMEM)
    return pl.pallas_call(
        kernel,
        out_shape=(jax.ShapeDtypeStruct((192, 512), F32), jax.ShapeDtypeStruct((192, 256), F32)),
        in_specs=[vmem] * 6,
        out_specs=(vmem, vmem),
        scratch_shapes=[
            pltpu.VMEM((4, 2, 256, 384), BF16),
            pltpu.VMEM((4, 8, 128), F32),
            pltpu.VMEM((4, 4, 192, 128), BF16),
            pltpu.VMEM((4, 4, 192, 128), BF16),
            pltpu.VMEM((192, 256), BF16),
            pltpu.VMEM((1, 128), jnp.int32),
            pltpu.VMEM((2048, 4096), BF16),
            pltpu.VMEM((2048, 128), F32),
            pltpu.VMEM((2, 8, 256), F32),
            pltpu.VMEM((2, 3, 8, 256), F32),
            pltpu.VMEM((2, 8, 256), F32),
            pltpu.VMEM((2, 7, 8, 256), F32),
            pltpu.VMEM((2, 192, 2048), BF16),
            pltpu.VMEM((8, 256, 192), F32),
            pltpu.VMEM((4, 256, 192), F32),
            pltpu.VMEM((4, 256, 192), F32),
            pltpu.VMEM((3, 256, 192), BF16),
            pltpu.VMEM((2, 128, 192), BF16),
            pltpu.VMEM((2, 256, 192), BF16),
            pltpu.SemaphoreType.DMA((len(NAMES),)),
            pltpu.SemaphoreType.DMA((len(NAMES),)),
        ],
        compiler_params=pltpu.CompilerParams(
            collective_id=0, has_side_effects=True, vmem_limit_bytes=52 * 1024 * 1024
        ),
    )(
        teacher_weight,
        student_weight,
        teacher_feats[0].T,
        student_feats[0].T,
        pairing,
        center.reshape(128, 128),
    )


def solution(mesh):
    columns = P(None, ("proto", "fsdp"))
    return jax.shard_map(
        shards,
        mesh=mesh,
        in_specs=(columns, columns, P("dp", "fsdp", None), P("dp", "fsdp", None), P("dp", "fsdp"), P("proto")),
        out_specs=(columns, P(None, ("proto", "fsdp", "dp"))),
        check_vma=False,
    )
```

time: 519 us -> 73.4 us (0.14)
  waiting for transfers between devices: 425 us -> 0 us
  Pallas kernels: 0 us -> 65.8 us
  matrix products: 38.4 us -> 0 us
  other arithmetic: 21 us -> 0 us
  blocking collectives: 14.4 us -> 0 us
  between operations: 13.8 us -> 0.65 us
    reduce_scatter x1 -> x0, waiting for transfers between devices: 299 us -> none  [shards(): lax.psum_scatter(lax.dot_general(derivs, z_student, (((0,), (0,)), ((), (...]
    all_gather x2 -> x0, waiting for transfers between devices: 126 us -> none  [the longest x1 65.5 us: shards(): lax.all_gather(w_student, 'fsdp', axis=1, tiled=True)]
    pallas_call x0 -> x1, Pallas kernels: none -> 65.8 us  [shards(): pl.pallas_call(kernel, out_shape=(jax.ShapeDtypeStruct((192, 512), F32),...]
    dot_general x3 -> x0, matrix products: 38.4 us -> none  [the longest x1 17.4 us: shards(): lax.dot_general(derivs, z_student, (((0,), (0,)), ((), ())), preferred_el...]
    reduce_sum x7 -> x0, other arithmetic: 17.2 us -> none  [the longest x1 12.2 us: shards(): jnp.sum(exp_s, axis=1)]
    pmax x1 -> x0, blocking collectives: 8.43 us -> none  [shards(): max_t, max_s = lax.pmax((local_max_t, local_max_s), 'proto')]
    psum x1 -> x0, blocking collectives: 6 us -> none  [shards(): lax.psum((jnp.sum(exp_t, axis=1), jnp.sum(exp_s, axis=1)), 'proto')]
    unnamed x9 -> x14, local copies, waits for them, and re-layouts: 1.01 us -> 6.71 us
  transfers between devices with their start and end apart: 4 -> 0, of which waited for: 3 -> 0; matrix products, arithmetic and copies ran while one was open for 3% -> 0% of each run, Pallas kernels for 0% -> 0%
where the time goes in v1:
time: 73.4 us; the launch traced here: 73.1 us
  Pallas kernels  65.8 us (90%)
  local copies, waits for them, and re-layouts  6.71 us (9%)
    pallas_call x1, Pallas kernels, shards(): pl.pallas_call(kernel, out_shape=(jax.ShapeDtypeStruct((192, 512), F32),...  65.8 us
    unnamed x14, local copies, waits for them, and re-layouts  6.71 us

profile of v1, /device:TPU:1, one launch (start us, length us, event | category | flops | bytes accessed | tf_op | source)
XLA Modules:
  0.0 73.1 jit_solution(12316250368781329098)
XLA Ops:
  0.6 0.0 copy-start.5
  0.6 0.7 copy-done.5
  1.3 0.0 copy-start
  1.3 1.0 %copy-done = f32[192,512]{1,0:T(8,128)S(1)} copy-done((f32[192,512]{1,0:T(8,128)S(1)}, f32[192,512]{1,0:T(8,128)}, u32[]{:S(2)}) %copy-start) | copy-done | bytes 393240
  2.3 0.0 copy-start.1
  2.3 1.0 %copy-done.1 = f32[192,512]{1,0:T(8,128)S(1)} copy-done((f32[192,512]{1,0:T(8,128)S(1)}, f32[192,512]{1,0:T(8,128)}, u32[]{:S(2)}) %copy-start.1) | copy-done | bytes 393240
  3.3 0.0 copy-start.2
  3.3 0.9 %copy-done.2 = bf16[1,256,192]{1,2,0:T(8,128)(2,1)S(1)} copy-done((bf16[1,256,192]{1,2,0:T(8,128)(2,1)S(1)}, bf16[1,256,192]{1,2,0:T(8,128)(2,1)}, u32[]{:S(2)}) %copy-start.2) | copy-done | bytes 98328
  4.2 0.0 copy-start.3
  4.2 0.9 %copy-done.3 = bf16[1,256,192]{1,2,0:T(8,128)(2,1)S(1)} copy-done((bf16[1,256,192]{1,2,0:T(8,128)(2,1)S(1)}, bf16[1,256,192]{1,2,0:T(8,128)(2,1)}, u32[]{:S(2)}) %copy-start.3) | copy-done | bytes 98328
  5.1 0.0 copy-start.4
  5.1 0.8 %copy-done.4 = f32[16384]{0:T(1024)S(1)} copy-done((f32[16384]{0:T(1024)S(1)}, f32[16384]{0:T(1024)}, u32[]{:S(2)}) %copy-start.4) | copy-done | bytes 65560
  5.9 65.8 %shard_map.77 = (f32[192,512]{1,0:T(8,128)S(1)}, f32[192,256]{1,0:T(8,128)S(1)}) custom-call(f32[192,512]{1,0:T(8,128)S(1)} %copy-done, f32[192,512]{1,0:T(8,128)S(1)} %copy-done.1, bf16[192,256]{1,0:T(8,128)(2,1)S(1)} %bitcast.7, bf16[192,256]{1,0:T(8,128)(2,1)S(1)} %bitcast.8, s32[1,256]{1,0:T(1,128)S(1)} %copy-done.5, f32[128,128]{1,0:T(8,128)S(1)} %bitcast.9), custom_call_target="tpu_custom_call" | custom-call | tf_op jit(solution)/shard_map/pallas_call | solution.py:402
  71.7 0.7 %copy.10 = f32[192,512]{1,0:T(8,128)} copy(f32[192,512]{1,0:T(8,128)S(1)} %get-tuple-element.4) | data formatting | bytes 786432
  72.4 0.7 copy.11
Async XLA Ops:
  0.6 0.7 copy-start.5
  1.3 1.0 %copy-start = (f32[192,512]{1,0:T(8,128)S(1)}, f32[192,512]{1,0:T(8,128)}, u32[]{:S(2)}) copy-start(f32[192,512]{1,0:T(8,128)} %tw_ref.1) | copy-start | bytes 1179652
  2.3 1.0 %copy-start.1 = (f32[192,512]{1,0:T(8,128)S(1)}, f32[192,512]{1,0:T(8,128)}, u32[]{:S(2)}) copy-start(f32[192,512]{1,0:T(8,128)} %sw_ref.1) | copy-start | bytes 1179652
  3.3 0.9 %copy-start.2 = (bf16[1,256,192]{1,2,0:T(8,128)(2,1)S(1)}, bf16[1,256,192]{1,2,0:T(8,128)(2,1)}, u32[]{:S(2)}) copy-start(bf16[1,256,192]{1,2,0:T(8,128)(2,1)} %param.8) | copy-start | bytes 294916
  4.2 0.9 %copy-start.3 = (bf16[1,256,192]{1,2,0:T(8,128)(2,1)S(1)}, bf16[1,256,192]{1,2,0:T(8,128)(2,1)}, u32[]{:S(2)}) copy-start(bf16[1,256,192]{1,2,0:T(8,128)(2,1)} %param.9) | copy-start | bytes 294916
  5.1 0.8 %copy-start.4 = (f32[16384]{0:T(1024)S(1)}, f32[16384]{0:T(1024)}, u32[]{:S(2)}) copy-start(f32[16384]{0:T(1024)} %param.11) | copy-start | bytes 196612

commit v2 on v0

v2 whole, which is shorter than its diff:
```python
import math

import jax
import jax.numpy as jnp
import numpy as np
from jax import lax
from jax.experimental import pallas as pl
from jax.experimental.pallas import tpu as pltpu
from jax.sharding import PartitionSpec as P

MESH = pl.DeviceIdType.MESH
F32, BF16 = jnp.float32, jnp.bfloat16
T_SCALE = math.log2(math.e) / 0.04
S_SCALE = math.log2(math.e) / 0.1
EPS = 1e-06


def rem(a, n):
    return lax.rem(a, np.int32(n))


def div(a, n):
    return lax.div(a, np.int32(n))


def device(x, y, z, core):
    return ((rem(x, 2) * 8 + z) * 2 + core, y, div(x, 2))


RECV = (
    [f"t{i}" for i in range(8)]
    + [f"s{i}" for i in range(8)]
    + ["wra", "wrb", "wla", "wlb", "wr2", "wl2"]
    + [f"ws{i}" for i in range(4)]
    + [f"c{i}" for i in range(1, 4)]
    + [f"x{i}" for i in range(1, 4)]
    + [f"z{i}" for i in range(1, 8)]
    + [f"g{i}" for i in range(4)]
    + [f"y{i}" for i in range(1, 4)]
)
RECV = {name: i for i, name in enumerate(RECV)}
SENDS = 128
LOADS = 6
ORDER = (0, 2, 6, 1, 7, 3, 5, 4)


def kernel(
    tw_hbm, sw_hbm, tf_hbm, sf_hbm, pair_hbm, cen_hbm, grad_ref, norm_ref,
    tw_ref, sw_ref, tf_ref, sf_ref, pair_ref, cen_ref,
    wbuf, cbuf, zs, zt, e_buf, cb, tot, xin, xsum, zin, factor, ag, at, gs_out, gs_in, ry_out, ry_in,
    ssem, rsem, lsem,
):
    f, y, d = lax.axis_index("fsdp"), lax.axis_index("proto"), lax.axis_index("dp")
    core, z = rem(f, 2), rem(div(f, 2), 8)
    x = d * 2 + div(f, 16)

    xs = [rem(x + k, 4) for k in range(4)]
    ys = [rem(y + k, 4) for k in range(4)]
    rows_z = [rem(z + k, 8) for k in range(8)]
    to_x = [device(xs[k], y, z, core) for k in range(4)]
    to_y = [device(x, ys[k], z, core) for k in range(4)]
    to_z = [device(x, y, rows_z[k], core) for k in range(8)]
    sibling = device(x, y, z, 1 - core)
    turn = rem(z + y + 8 - x, 4)
    at_turn = [turn == k for k in range(4)]

    def here(k, student):
        return at_turn[(-k + (0 if student else 2)) % 4]

    sent = []

    def send(when, name, src, dst, to):
        i = len(sent)
        pltpu.make_async_remote_copy(
            src_ref=src, dst_ref=dst, send_sem=ssem.at[i], recv_sem=rsem.at[RECV[name]], device_id=to, device_id_type=MESH
        ).start()
        sent.append((when, src.shape, src.dtype))

    def arrived(name, ref, offset=0):
        pltpu.make_async_remote_copy(
            src_ref=ref, dst_ref=ref, send_sem=ssem.at[0], recv_sem=rsem.at[RECV[name] + offset],
            device_id=sibling, device_id_type=MESH,
        ).wait_recv()

    peers = [sibling] + [to_y[k] for k in (1, 2, 3)] + [to_x[k] for k in (1, 2, 3)] + [to_z[k] for k in range(1, 8)]
    barrier = pltpu.get_barrier_semaphore()
    for peer in peers:
        pl.semaphore_signal(barrier, inc=1, device_id=peer, device_id_type=MESH)

    loads = [
        pltpu.make_async_copy(src, dst, lsem.at[i])
        for i, (src, dst) in enumerate(
            ((sf_hbm, sf_ref), (tf_hbm, tf_ref), (pair_hbm, pair_ref), (sw_hbm, sw_ref), (tw_hbm, tw_ref), (cen_hbm, cen_ref))
        )
    ]
    for load in loads:
        load.start()

    def normalized(feats_ref):
        feats = feats_ref[...].astype(F32)
        return (feats * lax.rsqrt(jnp.sum(feats * feats, axis=0, keepdims=True) + EPS)).astype(BF16)

    for load in loads[:3]:
        load.wait()

    @pl.when(here(0, True))
    def _():
        zs[z, 0:192] = normalized(sf_ref)
        zs[z, 192:208] = jnp.broadcast_to(pair_ref[...].astype(F32), (16, 256)).astype(BF16)

    @pl.when(here(0, False))
    def _():
        zt[z] = normalized(tf_ref)

    pl.semaphore_wait(barrier, len(peers))

    def block(student, k):
        return (zs if student else zt).at[rows_z[k % 8]]

    def name_of(student, k):
        return ("s" if student else "t") + str(k % 8)

    def along_x(when, student, k, steps=(2, 1, 3)):
        for i in steps:
            send(when, name_of(student, k), block(student, k), block(student, k), to_x[i])

    def along_z(when, student, steps, k=0):
        for i in steps:
            send(when, name_of(student, k - i), block(student, k), block(student, k), to_z[i])

    for student in (True, False):
        mine = here(0, student)

        @pl.when(mine)
        def _(student=student, mine=mine):
            along_x(mine, student, 0)
            along_z(mine, student, (2, 6, 3, 5, 4))

    for load in loads[3:]:
        load.wait()
    half = pl.ds(pl.multiple_of(d * 256, 256), 256)
    s_cols = sw_ref[:, half]
    t_cols = 0.994 * tw_ref[:, half] + 0.006 * s_cols
    ws = s_cols * lax.rsqrt(jnp.sum(s_cols * s_cols, axis=0, keepdims=True) + EPS)
    wt = t_cols * lax.rsqrt(jnp.sum(t_cols * t_cols, axis=0, keepdims=True) + EPS)
    wbuf[y, core] = jnp.concatenate([wt, ws], axis=0).T.astype(BF16)

    lowest = jnp.min(jnp.min(cen_ref[...], axis=0, keepdims=True), axis=1, keepdims=True)
    cbuf[y, 4:5, :] = jnp.broadcast_to(lowest, (1, 128))
    for k in range(4):
        row = 4 * (f - core) + 4 * (k // 2) + 2 * d + k % 2
        cbuf[y, k : k + 1, :] = cen_ref[pl.ds(row, 1), :]
    cbuf[y, 5:8, :] = jnp.zeros((3, 128), F32)

    first, last = pl.ds(0, 128), pl.ds(128, 128)
    own = wbuf.at[y, core]
    for name, part, k in (("wra", first, 1), ("wlb", last, 3), ("wrb", last, 1), ("wla", first, 3)):
        send(None, name, own.at[part], own.at[part], to_y[k])
    for k in (1, 3, 2):
        send(None, f"c{k}", cbuf.at[y], cbuf.at[y], to_y[k])
    send(None, "ws0", own, own, sibling)

    def forward(k):
        for student in (True, False):
            mine = here(k, student)

            @pl.when(mine)
            def _(student=student, mine=mine):
                arrived(name_of(student, k), block(student, k))
                along_x(mine, student, k)

    before, after = wbuf.at[ys[3], core], wbuf.at[ys[1], core]
    opposite = wbuf.at[ys[2], core]
    forward(2)
    forward(6)
    arrived("wra", before.at[first])
    send(None, "wr2", before.at[first], before.at[first], to_y[1])
    arrived("wlb", after.at[last])
    send(None, "wl2", after.at[last], after.at[last], to_y[3])

    forward(3)
    forward(5)
    arrived("wrb", before.at[last])
    send(None, "ws1", before, before, sibling)
    arrived("wla", after.at[first])
    send(None, "ws2", after, after, sibling)
    forward(4)
    for student in (True, False):

        @pl.when(jnp.logical_not(here(0, student)))
        def _(student=student):
            arrived(name_of(student, 0), block(student, 0))

        along_z(None, student, (1, 7))

    arrived("wr2", opposite.at[first])
    arrived("wl2", opposite.at[last])
    send(None, "ws3", opposite, opposite, sibling)

    for k in (1, 2, 3):
        arrived(f"c{k}", cbuf.at[ys[(4 - k) % 4]])
    floor = jnp.minimum(
        jnp.minimum(cbuf[0, 4:5, :], cbuf[1, 4:5, :]), jnp.minimum(cbuf[2, 4:5, :], cbuf[3, 4:5, :])
    )
    for k in range(16):
        row = (cbuf[k // 4, k % 4 : k % 4 + 1, :] - floor) * T_SCALE
        cb[k * 128 : (k + 1) * 128, :] = jnp.broadcast_to(row, (128, 128)).T

    for i, k in ((0, 0), (1, 3), (2, 1), (3, 2)):
        arrived(f"ws{i}", wbuf.at[ys[k], 1 - core])

    def scores(student, row, j):
        pad = jnp.zeros((64, 256), BF16)
        rhs = jnp.concatenate([pad, zs[row, 0:192]] if student else [zt[row], pad], axis=0)
        lanes = pl.ds(pl.multiple_of((2048 if student else 0) + j * 256, 256), 256)
        total = jnp.zeros((8, 256), F32)
        low = 128 if student else 0
        for m in range(8):
            rows = pl.ds(m * 256, 256)
            score = jnp.dot(wbuf[m // 2, m % 2, :, low : low + 256], rhs, preferred_element_type=F32)
            if student:
                value = jnp.exp2(score * S_SCALE)
            else:
                shift = cb[rows, :]
                value = jnp.exp2(score * T_SCALE - jnp.concatenate([shift, shift], axis=1))
            e_buf[rows, lanes] = value.astype(BF16)
            total = total + jnp.sum(value.reshape(32, 8, 256), axis=0)
        tot[1 if student else 0, pl.ds(row, 1), :] = jnp.sum(total, axis=0, keepdims=True)

    def offset(j):
        step = div(j + 1, 2)
        step = jnp.where(step == 1, 2, jnp.where(step == 2, 1, step))
        return jnp.where(rem(j, 2) == 1, step, rem(8 - step, 8))

    def chunk(j, _):
        k = offset(j)
        row = rem(z + k, 8)
        for student in (True, False):
            forwarded = rem(turn + k + (0 if student else 2), 4) == 0
            near = jnp.logical_or(k == 1, k == 7)

            @pl.when(jnp.logical_and(k != 0, jnp.logical_or(near, jnp.logical_not(forwarded))))
            def _(student=student):
                arrived("s0" if student else "t0", (zs if student else zt).at[row], k)

            scores(student, row, j)

    lax.fori_loop(0, 8, chunk, None)

    for i in (2, 1, 3):
        send(None, f"x{i}", tot, xin.at[i - 1], to_x[i])

    def paired(j, _):
        row = rem(z + offset(j), 8)
        names = jnp.broadcast_to(zs[row, 192:193].astype(F32), (256, 256))
        crops = lax.broadcasted_iota(jnp.int32, (256, 256), 0).astype(F32)
        onehot = jnp.where(names == crops, 1.0, 0.0).astype(BF16)
        ag[j] = lax.dot_general(
            zs[row, 0:192], onehot, (((1,), (1,)), ((), ())), preferred_element_type=F32
        )

    lax.fori_loop(0, 8, paired, None)
    for i in (1, 2, 3):
        arrived(f"x{i}", xin.at[i - 1])
    xsum[...] = tot[...] + xin[0] + xin[1] + xin[2]
    for i in (4, 3, 5, 2, 6, 1, 7):
        send(None, f"z{i}", xsum, zin.at[i - 1], to_z[i])
    for i in range(1, 8):
        arrived(f"z{i}", zin.at[i - 1])
    whole = xsum[...]
    for i in range(7):
        whole = whole + zin[i]
    factor[...] = 10.0 / whole
    for j in range(8):
        row = rows_z[ORDER[j]]
        at[:, j * 256 : (j + 1) * 256] = (ag[j] * -factor[0, pl.ds(row, 1), :]).astype(BF16)
        scaled = zs[row, 0:192].astype(F32) * factor[1, pl.ds(row, 1), :]
        at[:, 2048 + j * 256 : 2048 + (j + 1) * 256] = scaled.astype(BF16)

    def term(k, whose):
        m = ys[k] * 2 + whose
        return lax.dot_general(
            e_buf[pl.ds(pl.multiple_of(m * 256, 256), 256), :],
            at[...],
            (((1,), (1,)), ((), ())),
            preferred_element_type=F32,
        )

    def theirs(i, k):
        gs_out[i] = term(k, 1 - core)
        send(None, f"g{i}", gs_out.at[i], gs_in.at[i], sibling)

    def ours(i, k):
        part = term(k, core)
        arrived(f"g{i}", gs_in.at[i])
        part = part + gs_in[i]
        return jnp.concatenate([part, jnp.zeros((256, 64), F32)], axis=1).T[0:192]

    theirs(0, 2)
    theirs(1, 1)
    for i, k in enumerate((2, 1, 3)):
        ry_out[i] = ours(i, k).astype(BF16)
        send(None, f"y{k}", ry_out.at[i], ry_in.at[k - 1], to_y[k])
        if i < 2:
            theirs(i + 2, (3, 0)[i])
    total = ours(3, 0)
    for k in (2, 1, 3):
        arrived(f"y{k}", ry_in.at[k - 1])
        total = total + ry_in[k - 1].astype(F32)
    cols = sw_ref[:, half]
    norms = jnp.sqrt(jnp.sum(cols * cols, axis=0, keepdims=True) + EPS)
    unit = cols / norms
    grad_ref[...] = total - unit * jnp.sum(unit * total, axis=0, keepdims=True)
    norm_ref[...] = norms

    some = [
        zs.at[0], zt.at[0], wbuf.at[0, 0], wbuf.at[0, 0, first], cbuf.at[0], tot, gs_out.at[0],
    ]
    like = {(ref.shape, ref.dtype): ref for ref in some}
    for i, (when, shape, dtype) in enumerate(sent):
        ref = like[shape, dtype]

        def drain(i=i, ref=ref):
            pltpu.make_async_remote_copy(
                src_ref=ref, dst_ref=ref, send_sem=ssem.at[i], recv_sem=rsem.at[0], device_id=sibling, device_id_type=MESH
            ).wait_send()

        if when is None:
            drain()
        else:
            pl.when(when)(drain)


def shards(teacher_weight, student_weight, teacher_feats, student_feats, pairing, center):
    hbm = pl.BlockSpec(memory_space=pltpu.HBM)
    vmem = pl.BlockSpec(memory_space=pltpu.VMEM)
    scaled, norms = pl.pallas_call(
        kernel,
        out_shape=(jax.ShapeDtypeStruct((192, 256), F32), jax.ShapeDtypeStruct((1, 256), F32)),
        in_specs=[hbm] * 6,
        out_specs=(vmem, vmem),
        scratch_shapes=[
            pltpu.VMEM((192, 512), F32),
            pltpu.VMEM((192, 512), F32),
            pltpu.VMEM((192, 256), BF16),
            pltpu.VMEM((192, 256), BF16),
            pltpu.VMEM((1, 256), jnp.int32),
            pltpu.VMEM((128, 128), F32),
            pltpu.VMEM((4, 2, 256, 384), BF16),
            pltpu.VMEM((4, 8, 128), F32),
            pltpu.VMEM((8, 208, 256), BF16),
            pltpu.VMEM((8, 192, 256), BF16),
            pltpu.VMEM((2048, 4096), BF16),
            pltpu.VMEM((2048, 128), F32),
            pltpu.VMEM((2, 8, 256), F32),
            pltpu.VMEM((3, 2, 8, 256), F32),
            pltpu.VMEM((2, 8, 256), F32),
            pltpu.VMEM((7, 2, 8, 256), F32),
            pltpu.VMEM((2, 8, 256), F32),
            pltpu.VMEM((8, 192, 256), F32),
            pltpu.VMEM((192, 4096), BF16),
            pltpu.VMEM((4, 256, 192), F32),
            pltpu.VMEM((4, 256, 192), F32),
            pltpu.VMEM((3, 192, 256), BF16),
            pltpu.VMEM((3, 192, 256), BF16),
            pltpu.SemaphoreType.DMA((SENDS,)),
            pltpu.SemaphoreType.DMA((len(RECV),)),
            pltpu.SemaphoreType.DMA((LOADS,)),
        ],
        compiler_params=pltpu.CompilerParams(
            collective_id=0, has_side_effects=True, vmem_limit_bytes=60 * 1024 * 1024
        ),
    )(
        teacher_weight,
        student_weight,
        teacher_feats[0].T,
        student_feats[0].T,
        pairing,
        center.reshape(128, 128),
    )
    return 0.994 * teacher_weight + 0.006 * student_weight, scaled / norms


def solution(mesh):
    columns = P(None, ("proto", "fsdp"))
    return jax.shard_map(
        shards,
        mesh=mesh,
        in_specs=(columns, columns, P("dp", "fsdp", None), P("dp", "fsdp", None), P("dp", "fsdp"), P("proto")),
        out_specs=(columns, P(None, ("proto", "fsdp", "dp"))),
        check_vma=False,
    )
```

time: 519 us -> 61.7 us (0.12)
  waiting for transfers between devices: 425 us -> 0 us
  Pallas kernels: 0 us -> 58.4 us
  matrix products: 38.4 us -> 0 us
  other arithmetic: 21 us -> 2.51 us
  blocking collectives: 14.4 us -> 0 us
  between operations: 13.8 us -> 0.66 us
    reduce_scatter x1 -> x0, waiting for transfers between devices: 299 us -> none  [shards(): lax.psum_scatter(lax.dot_general(derivs, z_student, (((0,), (0,)), ((), (...]
    all_gather x2 -> x0, waiting for transfers between devices: 126 us -> none  [the longest x1 65.5 us: shards(): lax.all_gather(w_student, 'fsdp', axis=1, tiled=True)]
    pallas_call x0 -> x1, Pallas kernels: none -> 58.4 us  [shards(): pl.pallas_call(kernel, out_shape=(jax.ShapeDtypeStruct((192, 256), F32),...]
    dot_general x3 -> x0, matrix products: 38.4 us -> none  [the longest x1 17.4 us: shards(): lax.dot_general(derivs, z_student, (((0,), (0,)), ((), ())), preferred_el...]
    reduce_sum x7 -> x0, other arithmetic: 17.2 us -> none  [the longest x1 12.2 us: shards(): jnp.sum(exp_s, axis=1)]
    pmax x1 -> x0, blocking collectives: 8.43 us -> none  [shards(): max_t, max_s = lax.pmax((local_max_t, local_max_s), 'proto')]
    psum x1 -> x0, blocking collectives: 6 us -> none  [shards(): lax.psum((jnp.sum(exp_t, axis=1), jnp.sum(exp_s, axis=1)), 'proto')]
  transfers between devices with their start and end apart: 4 -> 0, of which waited for: 3 -> 0; matrix products, arithmetic and copies ran while one was open for 3% -> 0% of each run, Pallas kernels for 0% -> 0%
where the time goes in v2:
time: 61.7 us; the launch traced here: 61.5 us
  Pallas kernels  58.4 us (95%)
  other arithmetic  2.51 us (4%)
  between operations  0.66 us (1%)
    pallas_call x1, Pallas kernels, shards(): pl.pallas_call(kernel, out_shape=(jax.ShapeDtypeStruct((192, 256), F32),...  58.4 us
    div x1, other arithmetic, shards(): return (0.994 * teacher_weight + 0.006 * student_weight, scaled / norms)  1.68 us

profile of v2, /device:TPU:1, one launch (start us, length us, event | category | flops | bytes accessed | tf_op | source)
XLA Modules:
  0.0 61.5 jit_solution(13557314961820111281)
XLA Ops:
  0.6 0.0 copy-start.1
  0.6 58.4 %shard_map.77 = (f32[192,256]{1,0:T(8,128)}, f32[1,256]{1,0:T(1,128)}) custom-call(f32[192,512]{1,0:T(8,128)} %tw_hbm.1, f32[192,512]{1,0:T(8,128)} %sw_hbm.1, bf16[192,256]{1,0:T(8,128)(2,1)} %bitcast.8, bf16[192,256]{1,0:T(8,128)(2,1)} %bitcast.9, s32[1,256]{1,0:T(1,128)} %pair_hbm.1, f32[128,128]{1,0:T(8,128)} %bitcast.10), custom_call_target="tpu_custom_call" | custom-call | tf_op jit(solution)/shard_map/pallas_call | solution.py:337
  59.0 0.0 copy-start
  59.0 1.7 %broadcast_divide_fusion = f32[192,256]{1,0:T(8,128)} fusion(f32[192,256]{1,0:T(8,128)} %get-tuple-element.4, f32[256]{0:T(256)} %bitcast.11), kind=kLoop, calls=%fused_computation.1 | loop fusion | flops 49152 | bytes 394240 | tf_op jit(solution)/shard_map/div | solution.py:381
  60.7 0.0 copy-done.1
  60.7 0.0 copy-done
  60.7 0.8 %multiply_add_fusion = f32[192,512]{1,0:T(8,128)} fusion(f32[192,512]{1,0:T(8,128)S(1)} %copy-done, f32[192,512]{1,0:T(8,128)S(1)} %copy-done.1), kind=kLoop, calls=%fused_computation | loop fusion | flops 294912 | bytes 1179648 | tf_op jit(solution)/shard_map/add | solution.py:381
Async XLA Ops:
  0.6 60.1 %copy-start.1 = (f32[192,512]{1,0:T(8,128)S(1)}, f32[192,512]{1,0:T(8,128)}, u32[]{:S(2)}) copy-start(f32[192,512]{1,0:T(8,128)} %tw_hbm.1) | copy-start | bytes 1179652
  59.0 1.7 %copy-start = (f32[192,512]{1,0:T(8,128)S(1)}, f32[192,512]{1,0:T(8,128)}, u32[]{:S(2)}) copy-start(f32[192,512]{1,0:T(8,128)} %sw_hbm.1) | copy-start | bytes 1179652

commit v3 on v2

--- a/solution.py
+++ b/solution.py
@@ -33,21 +33,21 @@
     + ["wra", "wrb", "wla", "wlb", "wr2", "wl2"]
     + [f"ws{i}" for i in range(4)]
     + [f"c{i}" for i in range(1, 4)]
-    + [f"x{i}" for i in range(1, 4)]
-    + [f"z{i}" for i in range(1, 8)]
+    + [f"x{t}{i}" for t in range(2) for i in range(1, 4)]
+    + [f"z{t}{i}" for t in range(2) for i in range(1, 8)]
     + [f"g{i}" for i in range(4)]
     + [f"y{i}" for i in range(1, 4)]
 )
 RECV = {name: i for i, name in enumerate(RECV)}
 SENDS = 128
 LOADS = 6
-ORDER = (0, 2, 6, 1, 7, 3, 5, 4)
+ORDER = (0, 1, 7, 2, 6, 3, 5, 4)
 
 
 def kernel(
-    tw_hbm, sw_hbm, tf_hbm, sf_hbm, pair_hbm, cen_hbm, grad_ref, norm_ref,
+    tw_hbm, sw_hbm, tf_hbm, sf_hbm, pair_hbm, cen_hbm, grad_ref,
     tw_ref, sw_ref, tf_ref, sf_ref, pair_ref, cen_ref,
-    wbuf, cbuf, zs, zt, e_buf, cb, tot, xin, xsum, zin, factor, ag, at, gs_out, gs_in, ry_out, ry_in,
+    wbuf, cbuf, zs, zt, e_buf, cb, tot, xin, xsum, zin, factor, ag, at, g, gs_out, gs_in, ry_out, ry_in,
     ssem, rsem, lsem,
 ):
     f, y, d = lax.axis_index("fsdp"), lax.axis_index("proto"), lax.axis_index("dp")
@@ -173,6 +173,14 @@
     opposite = wbuf.at[ys[2], core]
     forward(2)
     forward(6)
+    for student in (True, False):
+
+        @pl.when(jnp.logical_not(here(0, student)))
+        def _(student=student):
+            arrived(name_of(student, 0), block(student, 0))
+
+        along_z(None, student, (1, 7))
+
     arrived("wra", before.at[first])
     send(None, "wr2", before.at[first], before.at[first], to_y[1])
     arrived("wlb", after.at[last])
@@ -185,14 +193,6 @@
     arrived("wla", after.at[first])
     send(None, "ws2", after, after, sibling)
     forward(4)
-    for student in (True, False):
-
-        @pl.when(jnp.logical_not(here(0, student)))
-        def _(student=student):
-            arrived(name_of(student, 0), block(student, 0))
-
-        along_z(None, student, (1, 7))
-
     arrived("wr2", opposite.at[first])
     arrived("wl2", opposite.at[last])
     send(None, "ws3", opposite, opposite, sibling)
@@ -229,26 +229,47 @@
 
     def offset(j):
         step = div(j + 1, 2)
-        step = jnp.where(step == 1, 2, jnp.where(step == 2, 1, step))
         return jnp.where(rem(j, 2) == 1, step, rem(8 - step, 8))
 
-    def chunk(j, _):
-        k = offset(j)
-        row = rem(z + k, 8)
-        for student in (True, False):
+    def chunk(student):
+        def body(j, _):
+            k = offset(j)
+            row = rem(z + k, 8)
             forwarded = rem(turn + k + (0 if student else 2), 4) == 0
             near = jnp.logical_or(k == 1, k == 7)
 
             @pl.when(jnp.logical_and(k != 0, jnp.logical_or(near, jnp.logical_not(forwarded))))
-            def _(student=student):
+            def _():
                 arrived("s0" if student else "t0", (zs if student else zt).at[row], k)
 
             scores(student, row, j)
 
-    lax.fori_loop(0, 8, chunk, None)
-
-    for i in (2, 1, 3):
-        send(None, f"x{i}", tot, xin.at[i - 1], to_x[i])
+        return body
+
+    def over_x(t):
+        for i in (2, 1, 3):
+            send(None, f"x{t}{i}", tot.at[t], xin.at[t, i - 1], to_x[i])
+
+    def over_z(t):
+        for i in (1, 2, 3):
+            arrived(f"x{t}{i}", xin.at[t, i - 1])
+        xsum[t] = tot[t] + xin[t, 0] + xin[t, 1] + xin[t, 2]
+        for i in (4, 3, 5, 2, 6, 1, 7):
+            send(None, f"z{t}{i}", xsum.at[t], zin.at[t, i - 1], to_z[i])
+
+    def totals(t):
+        for i in range(1, 8):
+            arrived(f"z{t}{i}", zin.at[t, i - 1])
+        whole = xsum[t]
+        for i in range(7):
+            whole = whole + zin[t, i]
+        factor[t] = 10.0 / whole
+
+    lax.fori_loop(0, 8, chunk(True), None)
+    over_x(1)
+    lax.fori_loop(0, 8, chunk(False), None)
+    over_x(0)
+    over_z(1)
 
     def paired(j, _):
         row = rem(z + offset(j), 8)
@@ -260,38 +281,40 @@
         )
 
     lax.fori_loop(0, 8, paired, None)
-    for i in (1, 2, 3):
-        arrived(f"x{i}", xin.at[i - 1])
-    xsum[...] = tot[...] + xin[0] + xin[1] + xin[2]
-    for i in (4, 3, 5, 2, 6, 1, 7):
-        send(None, f"z{i}", xsum, zin.at[i - 1], to_z[i])
-    for i in range(1, 8):
-        arrived(f"z{i}", zin.at[i - 1])
-    whole = xsum[...]
-    for i in range(7):
-        whole = whole + zin[i]
-    factor[...] = 10.0 / whole
+    over_z(0)
+    totals(1)
     for j in range(8):
         row = rows_z[ORDER[j]]
-        at[:, j * 256 : (j + 1) * 256] = (ag[j] * -factor[0, pl.ds(row, 1), :]).astype(BF16)
         scaled = zs[row, 0:192].astype(F32) * factor[1, pl.ds(row, 1), :]
-        at[:, 2048 + j * 256 : 2048 + (j + 1) * 256] = scaled.astype(BF16)
-
-    def term(k, whose):
-        m = ys[k] * 2 + whose
+        at[1, :, j * 256 : (j + 1) * 256] = scaled.astype(BF16)
+
+    def term(t, m):
         return lax.dot_general(
-            e_buf[pl.ds(pl.multiple_of(m * 256, 256), 256), :],
-            at[...],
+            e_buf[pl.ds(pl.multiple_of(m * 256, 256), 256), t * 2048 : (t + 1) * 2048],
+            at[t],
             (((1,), (1,)), ((), ())),
             preferred_element_type=F32,
         )
 
+    def student_term(m, _):
+        g[m] = term(1, m)
+
+    lax.fori_loop(0, 8, student_term, None)
+    totals(0)
+    for j in range(8):
+        row = rows_z[ORDER[j]]
+        at[0, :, j * 256 : (j + 1) * 256] = (ag[j] * -factor[0, pl.ds(row, 1), :]).astype(BF16)
+
+    def both(k, whose):
+        m = ys[k] * 2 + whose
+        return g[m] + term(0, m)
+
     def theirs(i, k):
-        gs_out[i] = term(k, 1 - core)
+        gs_out[i] = both(k, 1 - core)
         send(None, f"g{i}", gs_out.at[i], gs_in.at[i], sibling)
 
     def ours(i, k):
-        part = term(k, core)
+        part = both(k, core)
         arrived(f"g{i}", gs_in.at[i])
         part = part + gs_in[i]
         return jnp.concatenate([part, jnp.zeros((256, 64), F32)], axis=1).T[0:192]
@@ -299,10 +322,11 @@
     theirs(0, 2)
     theirs(1, 1)
     for i, k in enumerate((2, 1, 3)):
+        if i == 0:
+            theirs(2, 3)
         ry_out[i] = ours(i, k).astype(BF16)
         send(None, f"y{k}", ry_out.at[i], ry_in.at[k - 1], to_y[k])
-        if i < 2:
-            theirs(i + 2, (3, 0)[i])
+    theirs(3, 0)
     total = ours(3, 0)
     for k in (2, 1, 3):
         arrived(f"y{k}", ry_in.at[k - 1])
@@ -310,11 +334,10 @@
     cols = sw_ref[:, half]
     norms = jnp.sqrt(jnp.sum(cols * cols, axis=0, keepdims=True) + EPS)
     unit = cols / norms
-    grad_ref[...] = total - unit * jnp.sum(unit * total, axis=0, keepdims=True)
-    norm_ref[...] = norms
+    grad_ref[...] = (total - unit * jnp.sum(unit * total, axis=0, keepdims=True)) / norms
 
     some = [
-        zs.at[0], zt.at[0], wbuf.at[0, 0], wbuf.at[0, 0, first], cbuf.at[0], tot, gs_out.at[0],
+        zs.at[0], zt.at[0], wbuf.at[0, 0], wbuf.at[0, 0, first], cbuf.at[0], tot.at[0], gs_out.at[0],
     ]
     like = {(ref.shape, ref.dtype): ref for ref in some}
     for i, (when, shape, dtype) in enumerate(sent):
@@ -334,11 +357,11 @@
 def shards(teacher_weight, student_weight, teacher_feats, student_feats, pairing, center):
     hbm = pl.BlockSpec(memory_space=pltpu.HBM)
     vmem = pl.BlockSpec(memory_space=pltpu.VMEM)
-    scaled, norms = pl.pallas_call(
+    student_grad = pl.pallas_call(
         kernel,
-        out_shape=(jax.ShapeDtypeStruct((192, 256), F32), jax.ShapeDtypeStruct((1, 256), F32)),
+        out_shape=jax.ShapeDtypeStruct((192, 256), F32),
         in_specs=[hbm] * 6,
-        out_specs=(vmem, vmem),
+        out_specs=vmem,
         scratch_shapes=[
             pltpu.VMEM((192, 512), F32),
             pltpu.VMEM((192, 512), F32),
@@ -353,12 +376,13 @@
             pltpu.VMEM((2048, 4096), BF16),
             pltpu.VMEM((2048, 128), F32),
             pltpu.VMEM((2, 8, 256), F32),
-            pltpu.VMEM((3, 2, 8, 256), F32),
+            pltpu.VMEM((2, 3, 8, 256), F32),
             pltpu.VMEM((2, 8, 256), F32),
-            pltpu.VMEM((7, 2, 8, 256), F32),
+            pltpu.VMEM((2, 7, 8, 256), F32),
             pltpu.VMEM((2, 8, 256), F32),
             pltpu.VMEM((8, 192, 256), F32),
-            pltpu.VMEM((192, 4096), BF16),
+            pltpu.VMEM((2, 192, 2048), BF16),
+            pltpu.VMEM((8, 256, 192), F32),
             pltpu.VMEM((4, 256, 192), F32),
             pltpu.VMEM((4, 256, 192), F32),
             pltpu.VMEM((3, 192, 256), BF16),
@@ -378,7 +402,7 @@
         pairing,
         center.reshape(128, 128),
     )
-    return 0.994 * teacher_weight + 0.006 * student_weight, scaled / norms
+    return 0.994 * teacher_weight + 0.006 * student_weight, student_grad
 
 
 def solution(mesh):

time: 61.7 us -> 57.8 us (0.937)
  Pallas kernels: 58.4 us -> 55.4 us
  other arithmetic: 2.51 us -> 0.82 us
  local copies, waits for them, and re-layouts: 0.01 us -> 0.78 us
    pallas_call x1, Pallas kernels: 58.4 us -> 55.4 us  [shards(): pl.pallas_call(kernel, out_shape=jax.ShapeDtypeStruct((192, 256), F32), i...]
    div x1 -> x0, other arithmetic: 1.68 us -> none  [shards(): return (0.994 * teacher_weight + 0.006 * student_weight, scaled / norms)]
    unnamed x4 -> x7, local copies, waits for them, and re-layouts: 0.01 us -> 0.78 us
where the time goes in v3:
time: 57.8 us; the launch traced here: 57.7 us
  Pallas kernels  55.4 us (96%)
  other arithmetic  0.82 us (1%)
  local copies, waits for them, and re-layouts  0.78 us (1%)
  between operations  0.68 us (1%)
    pallas_call x1, Pallas kernels, shards(): pl.pallas_call(kernel, out_shape=jax.ShapeDtypeStruct((192, 256), F32), i...  55.4 us

profile of v3, /device:TPU:1, one launch (start us, length us, event | category | flops | bytes accessed | tf_op | source)
XLA Modules:
  0.0 57.7 jit_solution(14852626857876771559)
XLA Ops:
  0.6 0.0 copy-start
  0.6 0.0 copy-start.1
  0.7 55.4 %shard_map.77 = f32[192,256]{1,0:T(8,128)} custom-call(f32[192,512]{1,0:T(8,128)} %tw_hbm.1, f32[192,512]{1,0:T(8,128)} %sw_hbm.1, bf16[192,256]{1,0:T(8,128)(2,1)} %bitcast.7, bf16[192,256]{1,0:T(8,128)(2,1)} %bitcast.8, s32[1,256]{1,0:T(1,128)} %pair_hbm.1, f32[128,128]{1,0:T(8,128)} %bitcast.9), custom_call_target="tpu_custom_call" | custom-call | tf_op jit(solution)/shard_map/pallas_call | solution.py:360
  56.1 0.0 copy-done
  56.1 0.0 copy-done.1
  56.1 0.0 copy-start.2
  56.1 0.8 %multiply_add_fusion = f32[192,512]{1,0:T(8,128)} fusion(f32[192,512]{1,0:T(8,128)S(1)} %copy-done, f32[192,512]{1,0:T(8,128)S(1)} %copy-done.1), kind=kLoop, calls=%fused_computation | loop fusion | flops 294912 | bytes 1179648 | tf_op jit(solution)/shard_map/add | solution.py:405
  56.9 0.1 copy-done.2
  57.0 0.7 %copy.9 = f32[192,256]{1,0:T(8,128)} copy(f32[192,256]{1,0:T(8,128)S(1)} %copy-done.2) | data formatting | bytes 393216
Async XLA Ops:
  0.6 55.5 %copy-start = (f32[192,512]{1,0:T(8,128)S(1)}, f32[192,512]{1,0:T(8,128)}, u32[]{:S(2)}) copy-start(f32[192,512]{1,0:T(8,128)} %sw_hbm.1) | copy-start | bytes 1179652
  0.6 55.5 %copy-start.1 = (f32[192,512]{1,0:T(8,128)S(1)}, f32[192,512]{1,0:T(8,128)}, u32[]{:S(2)}) copy-start(f32[192,512]{1,0:T(8,128)} %tw_hbm.1) | copy-start | bytes 1179652
  56.1 0.9 %copy-start.2 = (f32[192,256]{1,0:T(8,128)S(1)}, f32[192,256]{1,0:T(8,128)}, u32[]{:S(2)}) copy-start(f32[192,256]{1,0:T(8,128)} %shard_map.77) | copy-start | bytes 589828

commit v4 on v3

--- a/solution.py
+++ b/solution.py
@@ -134,7 +134,7 @@
         @pl.when(mine)
         def _(student=student, mine=mine):
             along_x(mine, student, 0)
-            along_z(mine, student, (2, 6, 3, 5, 4))
+            along_z(mine, student, (2, 6, 3, 5, 4) if student else (2, 6))
 
     for load in loads[3:]:
         load.wait()
@@ -167,7 +167,19 @@
             @pl.when(mine)
             def _(student=student, mine=mine):
                 arrived(name_of(student, k), block(student, k))
-                along_x(mine, student, k)
+                if not student and k == 2:
+                    along_z(mine, student, (7, 6), k)
+                if not student and k == 6:
+                    along_z(mine, student, (1,), k)
+                along_x(mine, student, k, (2, 1, 3) if student or k == 4 else (3, 1))
+
+    def relay(k):
+        mine = here(k - 1, False)
+
+        @pl.when(mine)
+        def _():
+            arrived(name_of(False, k), block(False, k))
+            along_x(mine, False, k, (3,))
 
     before, after = wbuf.at[ys[3], core], wbuf.at[ys[1], core]
     opposite = wbuf.at[ys[2], core]
@@ -193,6 +205,8 @@
     arrived("wla", after.at[first])
     send(None, "ws2", after, after, sibling)
     forward(4)
+    relay(2)
+    relay(6)
     arrived("wr2", opposite.at[first])
     arrived("wl2", opposite.at[last])
     send(None, "ws3", opposite, opposite, sibling)
@@ -236,6 +250,9 @@
             k = offset(j)
             row = rem(z + k, 8)
             forwarded = rem(turn + k + (0 if student else 2), 4) == 0
+            if not student:
+                relayed = jnp.logical_and(rem(turn + k + 1, 4) == 0, k != 4)
+                forwarded = jnp.logical_or(forwarded, relayed)
             near = jnp.logical_or(k == 1, k == 7)
 
             @pl.when(jnp.logical_and(k != 0, jnp.logical_or(near, jnp.logical_not(forwarded))))
@@ -265,7 +282,10 @@
             whole = whole + zin[t, i]
         factor[t] = 10.0 / whole
 
-    lax.fori_loop(0, 8, chunk(True), None)
+    lax.fori_loop(0, 5, chunk(True), None)
+    relay(3)
+    relay(5)
+    lax.fori_loop(5, 8, chunk(True), None)
     over_x(1)
     lax.fori_loop(0, 8, chunk(False), None)
     over_x(0)

time: 57.8 us -> 55.4 us (0.958)
  Pallas kernels: 55.4 us -> 53 us
    pallas_call x1, Pallas kernels: 55.4 us -> 53 us  [shards(): pl.pallas_call(kernel, out_shape=jax.ShapeDtypeStruct((192, 256), F32), i...]
where the time goes in v4:
time: 55.4 us; the launch traced here: 55.3 us
  Pallas kernels  53 us (96%)
  other arithmetic  0.82 us (1%)
  local copies, waits for them, and re-layouts  0.78 us (1%)
  between operations  0.68 us (1%)
    pallas_call x1, Pallas kernels, shards(): pl.pallas_call(kernel, out_shape=jax.ShapeDtypeStruct((192, 256), F32), i...  53 us

profile of v4, /device:TPU:1, one launch (start us, length us, event | category | flops | bytes accessed | tf_op | source)
XLA Modules:
  0.0 55.3 jit_solution(14415257320759116679)
XLA Ops:
  0.6 0.0 copy-start
  0.6 0.0 copy-start.1
  0.7 53.0 %shard_map.77 = f32[192,256]{1,0:T(8,128)} custom-call(f32[192,512]{1,0:T(8,128)} %tw_hbm.1, f32[192,512]{1,0:T(8,128)} %sw_hbm.1, bf16[192,256]{1,0:T(8,128)(2,1)} %bitcast.7, bf16[192,256]{1,0:T(8,128)(2,1)} %bitcast.8, s32[1,256]{1,0:T(1,128)} %pair_hbm.1, f32[128,128]{1,0:T(8,128)} %bitcast.9), custom_call_target="tpu_custom_call" | custom-call | tf_op jit(solution)/shard_map/pallas_call | solution.py:380
  53.6 0.0 copy-done
  53.6 0.0 copy-done.1
  53.7 0.0 copy-start.2
  53.7 0.8 %multiply_add_fusion = f32[192,512]{1,0:T(8,128)} fusion(f32[192,512]{1,0:T(8,128)S(1)} %copy-done, f32[192,512]{1,0:T(8,128)S(1)} %copy-done.1), kind=kLoop, calls=%fused_computation | loop fusion | flops 294912 | bytes 1179648 | tf_op jit(solution)/shard_map/add | solution.py:425
  54.5 0.1 copy-done.2
  54.6 0.7 %copy.9 = f32[192,256]{1,0:T(8,128)} copy(f32[192,256]{1,0:T(8,128)S(1)} %copy-done.2) | data formatting | bytes 393216
Async XLA Ops:
  0.6 53.0 %copy-start = (f32[192,512]{1,0:T(8,128)S(1)}, f32[192,512]{1,0:T(8,128)}, u32[]{:S(2)}) copy-start(f32[192,512]{1,0:T(8,128)} %sw_hbm.1) | copy-start | bytes 1179652
  0.6 53.0 %copy-start.1 = (f32[192,512]{1,0:T(8,128)S(1)}, f32[192,512]{1,0:T(8,128)}, u32[]{:S(2)}) copy-start(f32[192,512]{1,0:T(8,128)} %tw_hbm.1) | copy-start | bytes 1179652
  53.7 0.9 %copy-start.2 = (f32[192,256]{1,0:T(8,128)S(1)}, f32[192,256]{1,0:T(8,128)}, u32[]{:S(2)}) copy-start(f32[192,256]{1,0:T(8,128)} %shard_map.77) | copy-start | bytes 589828

commit v5 on v4

--- a/solution.py
+++ b/solution.py
@@ -134,7 +134,7 @@
         @pl.when(mine)
         def _(student=student, mine=mine):
             along_x(mine, student, 0)
-            along_z(mine, student, (2, 6, 3, 5, 4) if student else (2, 6))
+            along_z(mine, student, (2, 6))
 
     for load in loads[3:]:
         load.wait()
@@ -167,10 +167,10 @@
             @pl.when(mine)
             def _(student=student, mine=mine):
                 arrived(name_of(student, k), block(student, k))
-                if not student and k == 2:
-                    along_z(mine, student, (7, 6), k)
-                if not student and k == 6:
-                    along_z(mine, student, (1,), k)
+                if k == 2:
+                    along_z(mine, student, (7,) if student else (7, 6), k)
+                if k == 6:
+                    along_z(mine, student, (1, 2) if student else (1,), k)
                 along_x(mine, student, k, (2, 1, 3) if student or k == 4 else (3, 1))
 
     def relay(k):
@@ -197,6 +197,15 @@
     send(None, "wr2", before.at[first], before.at[first], to_y[1])
     arrived("wlb", after.at[last])
     send(None, "wl2", after.at[last], after.at[last], to_y[3])
+
+    for k in (1, 2, 3):
+        arrived(f"c{k}", cbuf.at[ys[(4 - k) % 4]])
+    floor = jnp.minimum(
+        jnp.minimum(cbuf[0, 4:5, :], cbuf[1, 4:5, :]), jnp.minimum(cbuf[2, 4:5, :], cbuf[3, 4:5, :])
+    )
+    for k in range(16):
+        row = (cbuf[k // 4, k % 4 : k % 4 + 1, :] - floor) * T_SCALE
+        cb[k * 128 : (k + 1) * 128, :] = jnp.broadcast_to(row, (128, 128)).T
 
     forward(3)
     forward(5)
@@ -210,15 +219,6 @@
     arrived("wr2", opposite.at[first])
     arrived("wl2", opposite.at[last])
     send(None, "ws3", opposite, opposite, sibling)
-
-    for k in (1, 2, 3):
-        arrived(f"c{k}", cbuf.at[ys[(4 - k) % 4]])
-    floor = jnp.minimum(
-        jnp.minimum(cbuf[0, 4:5, :], cbuf[1, 4:5, :]), jnp.minimum(cbuf[2, 4:5, :], cbuf[3, 4:5, :])
-    )
-    for k in range(16):
-        row = (cbuf[k // 4, k % 4 : k % 4 + 1, :] - floor) * T_SCALE
-        cb[k * 128 : (k + 1) * 128, :] = jnp.broadcast_to(row, (128, 128)).T
 
     for i, k in ((0, 0), (1, 3), (2, 1), (3, 2)):
         arrived(f"ws{i}", wbuf.at[ys[k], 1 - core])
@@ -282,10 +282,10 @@
             whole = whole + zin[t, i]
         factor[t] = 10.0 / whole
 
-    lax.fori_loop(0, 5, chunk(True), None)
+    lax.fori_loop(0, 6, chunk(True), None)
     relay(3)
     relay(5)
-    lax.fori_loop(5, 8, chunk(True), None)
+    lax.fori_loop(6, 8, chunk(True), None)
     over_x(1)
     lax.fori_loop(0, 8, chunk(False), None)
     over_x(0)

time: 55.4 us -> 54.6 us (0.986)
  Pallas kernels: 53 us -> 52.2 us
    pallas_call x1, Pallas kernels: 53 us -> 52.2 us  [shards(): pl.pallas_call(kernel, out_shape=jax.ShapeDtypeStruct((192, 256), F32), i...]
where the time goes in v5:
time: 54.6 us; the launch traced here: 54.5 us
  Pallas kernels  52.2 us (96%)
  other arithmetic  0.82 us (2%)
  local copies, waits for them, and re-layouts  0.78 us (1%)
  between operations  0.68 us (1%)
    pallas_call x1, Pallas kernels, shards(): pl.pallas_call(kernel, out_shape=jax.ShapeDtypeStruct((192, 256), F32), i...  52.2 us

profile of v5, /device:TPU:1, one launch (start us, length us, event | category | flops | bytes accessed | tf_op | source)
XLA Modules:
  0.0 54.5 jit_solution(6972507203830963707)
XLA Ops:
  0.6 0.0 copy-start
  0.6 0.0 copy-start.1
  0.7 52.2 %shard_map.77 = f32[192,256]{1,0:T(8,128)} custom-call(f32[192,512]{1,0:T(8,128)} %tw_hbm.1, f32[192,512]{1,0:T(8,128)} %sw_hbm.1, bf16[192,256]{1,0:T(8,128)(2,1)} %bitcast.7, bf16[192,256]{1,0:T(8,128)(2,1)} %bitcast.8, s32[1,256]{1,0:T(1,128)} %pair_hbm.1, f32[128,128]{1,0:T(8,128)} %bitcast.9), custom_call_target="tpu_custom_call" | custom-call | tf_op jit(solution)/shard_map/pallas_call | solution.py:380
  52.9 0.0 copy-done
  52.9 0.0 copy-done.1
  52.9 0.0 copy-start.2
  52.9 0.8 %multiply_add_fusion = f32[192,512]{1,0:T(8,128)} fusion(f32[192,512]{1,0:T(8,128)S(1)} %copy-done, f32[192,512]{1,0:T(8,128)S(1)} %copy-done.1), kind=kLoop, calls=%fused_computation | loop fusion | flops 294912 | bytes 1179648 | tf_op jit(solution)/shard_map/add | solution.py:425
  53.7 0.1 copy-done.2
  53.8 0.7 %copy.9 = f32[192,256]{1,0:T(8,128)} copy(f32[192,256]{1,0:T(8,128)S(1)} %copy-done.2) | data formatting | bytes 393216
Async XLA Ops:
  0.6 52.2 %copy-start = (f32[192,512]{1,0:T(8,128)S(1)}, f32[192,512]{1,0:T(8,128)}, u32[]{:S(2)}) copy-start(f32[192,512]{1,0:T(8,128)} %sw_hbm.1) | copy-start | bytes 1179652
  0.6 52.2 %copy-start.1 = (f32[192,512]{1,0:T(8,128)S(1)}, f32[192,512]{1,0:T(8,128)}, u32[]{:S(2)}) copy-start(f32[192,512]{1,0:T(8,128)} %tw_hbm.1) | copy-start | bytes 1179652
  52.9 0.9 %copy-start.2 = (f32[192,256]{1,0:T(8,128)S(1)}, f32[192,256]{1,0:T(8,128)}, u32[]{:S(2)}) copy-start(f32[192,256]{1,0:T(8,128)} %shard_map.77) | copy-start | bytes 589828

commit v6 on v5

--- a/solution.py
+++ b/solution.py
@@ -185,7 +185,7 @@
     opposite = wbuf.at[ys[2], core]
     forward(2)
     forward(6)
-    for student in (True, False):
+    for student in (True,):
 
         @pl.when(jnp.logical_not(here(0, student)))
         def _(student=student):
@@ -214,6 +214,14 @@
     arrived("wla", after.at[first])
     send(None, "ws2", after, after, sibling)
     forward(4)
+    for student in (False,):
+
+        @pl.when(jnp.logical_not(here(0, student)))
+        def _(student=student):
+            arrived(name_of(student, 0), block(student, 0))
+
+        along_z(None, student, (1, 7))
+
     relay(2)
     relay(6)
     arrived("wr2", opposite.at[first])

time: 54.6 us -> 54.7 us (level)
  no operation moved by 1% of the time
where the time goes in v6:
time: 54.7 us; the launch traced here: 54.6 us
  Pallas kernels  52.3 us (96%)
  other arithmetic  0.82 us (1%)
  local copies, waits for them, and re-layouts  0.78 us (1%)
  between operations  0.68 us (1%)
    pallas_call x1, Pallas kernels, shards(): pl.pallas_call(kernel, out_shape=jax.ShapeDtypeStruct((192, 256), F32), i...  52.3 us

profile of v6, /device:TPU:1, one launch (start us, length us, event | category | flops | bytes accessed | tf_op | source)
XLA Modules:
  0.0 54.6 jit_solution(5264510692806588578)
XLA Ops:
  0.6 0.0 copy-start
  0.6 0.0 copy-start.1
  0.7 52.3 %shard_map.77 = f32[192,256]{1,0:T(8,128)} custom-call(f32[192,512]{1,0:T(8,128)} %tw_hbm.1, f32[192,512]{1,0:T(8,128)} %sw_hbm.1, bf16[192,256]{1,0:T(8,128)(2,1)} %bitcast.7, bf16[192,256]{1,0:T(8,128)(2,1)} %bitcast.8, s32[1,256]{1,0:T(1,128)} %pair_hbm.1, f32[128,128]{1,0:T(8,128)} %bitcast.9), custom_call_target="tpu_custom_call" | custom-call | tf_op jit(solution)/shard_map/pallas_call | solution.py:388
  53.0 0.0 copy-done
  53.0 0.0 copy-done.1
  53.0 0.0 copy-start.2
  53.0 0.8 %multiply_add_fusion = f32[192,512]{1,0:T(8,128)} fusion(f32[192,512]{1,0:T(8,128)S(1)} %copy-done, f32[192,512]{1,0:T(8,128)S(1)} %copy-done.1), kind=kLoop, calls=%fused_computation | loop fusion | flops 294912 | bytes 1179648 | tf_op jit(solution)/shard_map/add | solution.py:433
  53.8 0.1 copy-done.2
  53.9 0.7 %copy.9 = f32[192,256]{1,0:T(8,128)} copy(f32[192,256]{1,0:T(8,128)S(1)} %copy-done.2) | data formatting | bytes 393216
Async XLA Ops:
  0.6 52.3 %copy-start = (f32[192,512]{1,0:T(8,128)S(1)}, f32[192,512]{1,0:T(8,128)}, u32[]{:S(2)}) copy-start(f32[192,512]{1,0:T(8,128)} %sw_hbm.1) | copy-start | bytes 1179652
  0.6 52.3 %copy-start.1 = (f32[192,512]{1,0:T(8,128)S(1)}, f32[192,512]{1,0:T(8,128)}, u32[]{:S(2)}) copy-start(f32[192,512]{1,0:T(8,128)} %tw_hbm.1) | copy-start | bytes 1179652
  53.0 0.9 %copy-start.2 = (f32[192,256]{1,0:T(8,128)S(1)}, f32[192,256]{1,0:T(8,128)}, u32[]{:S(2)}) copy-start(f32[192,256]{1,0:T(8,128)} %shard_map.77) | copy-start | bytes 589828
